TPU v7x, 512 devices: a whole 4x4x16 slice. The times are simulated.
512 devices in a mesh: wide: 32 (over x, z_hi, core), narrow: 16 (over y, z_lo).
Axes of the slice: x: 4, y: 4, z: 16 (z_hi: 4, z_lo: 4; z = z_hi * 4 + z_lo), core: 2. Of those that a mesh axis runs over, the one named last changes fastest.
Arguments:
- features: bfloat16 [262144, 512], P(('wide', 'narrow')), may hold values from -6 to 6
- stripe_owner: int32 [16, 2], replicated, may hold values from 0 to 31
- dense_weight: int32 [262144, 1024], P(('wide', 'narrow')), may hold values from 0 to 3
- sparse_weight: int32 [512, 16, 128, 128], P(('wide', 'narrow')), may hold values from 0 to 3
- send_blocks: int32 [512, 16, 2], P(('wide', 'narrow')), may hold values from -1 to 3, as said below
- target_block: int32 [512, 16, 2], P(('wide', 'narrow')), may hold values from 0 to 3
- first_weight: bfloat16 [512, 2048], P('wide'), may hold values from -0.25 to 0.25
- second_weight: bfloat16 [2048, 512], P('wide'), may hold values from -0.125 to 0.125
Outputs:
- updated: bfloat16 [262144, 512], P(('wide', 'narrow'))
Inputs may be any that keep to these rules, and one draw needn't show every extreme that they name: `send_blocks`: entry [d, p, s] names a local row block of device d for slot s to partition p of d's wide group, -1 marks an empty slot, filled slots come first; in every wide group one partition receives 2 blocks from every member.
All inputs are finite; a program needn't handle non-finite values.
Results may differ from a plain program's by a relative error of at most 0.0057.
Values may be sent and summed in bfloat16 or wider, within the bound.
A program may use at most 128 MiB of HBM per device.

v0:
```python
import jax
import jax.numpy as jnp
from jax import lax
from jax.sharding import PartitionSpec as P


def padded_to(lines, count):
    spare = -len(lines) % count
    return jnp.pad(lines, [(0, spare)] + [(0, 0)] * (lines.ndim - 1))


def total_of(x, axis):
    lines = x.reshape(-1, *x.shape[1:][-1:])
    padded = padded_to(lines, lax.axis_size(axis))
    own = lax.psum_scatter(padded, axis, scatter_dimension=0, tiled=True)
    whole = lax.all_gather(own, axis, axis=0, tiled=True)
    return whole[: len(lines)].reshape(x.shape)


def tile_products(tile_weights, received):
    carried, present = received
    products = jnp.einsum(
        "pij,pcjd->pcid", tile_weights, carried, preferred_element_type=jnp.float32
    )
    return (products, present)


def add_rows(left, portion):
    return jnp.dot(left, portion, preferred_element_type=jnp.float32)


def shards(
    features,
    stripe_owner,
    dense_weight,
    sparse_weight,
    send_blocks,
    target_block,
    first_weight,
    second_weight,
):
    row_count, feature_width = features.shape
    block_rows = sparse_weight.shape[2]
    blocks_dev = row_count // block_rows
    stripe_count = stripe_owner.shape[1]
    narrow_index = lax.axis_index("narrow")
    wide_index = lax.axis_index("wide")
    owners = lax.dynamic_index_in_dim(stripe_owner, narrow_index, 0, keepdims=False)
    wide_rows = features.astype(jnp.float32)
    masked = jnp.stack(
        [
            jnp.where(owners[stripe_index] == wide_index, wide_rows, 0.0)
            for stripe_index in range(stripe_count)
        ]
    )
    stripes = (
        total_of(masked.astype(jnp.bfloat16), "wide")
        .astype(jnp.float32)
        .astype(jnp.bfloat16)
        .reshape(stripe_count * row_count, feature_width)
    )
    dense_sum = jnp.dot(
        dense_weight.astype(jnp.bfloat16), stripes, preferred_element_type=jnp.float32
    )
    tile_weights = sparse_weight[0].astype(jnp.bfloat16)
    listed = send_blocks[0]
    present = listed >= 0
    block_grid = features.reshape(blocks_dev, block_rows, feature_width)
    chosen = jnp.take(block_grid, jnp.maximum(listed, 0), axis=0)
    chosen = jnp.where(present[:, :, None, None], chosen, jnp.zeros((), jnp.bfloat16))
    products, arrived = tile_products(
        tile_weights,
        (
            lax.all_to_all(chosen, "narrow", split_axis=0, concat_axis=0, tiled=True),
            lax.all_to_all(
                present.astype(jnp.bfloat16), "narrow", split_axis=0, concat_axis=0, tiled=True
            ),
        ),
    )
    highest = lax.Precision.HIGHEST
    routed = (target_block[0][:, :, None] == jnp.arange(blocks_dev)[None, None, :]) & (
        arrived[:, :, None] > 0.5
    )
    routed = routed.astype(jnp.float32)
    sparse_sum = jnp.einsum("pcb,pcid->bid", routed, products, precision=highest).reshape(
        row_count, feature_width
    )
    row_weight = jnp.sum(sparse_weight[0], axis=2).astype(jnp.float32)
    sparse_degree = jnp.einsum("pcb,pi->bi", routed, row_weight, precision=highest).reshape(
        row_count
    )
    degree = 1.0 + jnp.sum(dense_weight, axis=1).astype(jnp.float32) + sparse_degree
    combined = (
        features.astype(jnp.float32) + (dense_sum + sparse_sum) / jnp.sqrt(degree)[:, None]
    ).astype(jnp.bfloat16)
    gated = add_rows(combined, lax.all_gather(first_weight, "wide", axis=0, tiled=True))
    hidden = jax.nn.relu(gated).astype(jnp.bfloat16)
    updated = add_rows(hidden, lax.all_gather(second_weight, "wide", axis=0, tiled=True))
    return updated.astype(jnp.bfloat16)


def solution(mesh):
    placed = (
        P(("wide", "narrow"), None),
        P(),
        P(("wide", "narrow"), None),
        P(("wide", "narrow"), None, None, None),
        P(("wide", "narrow"), None, None),
        P(("wide", "narrow"), None, None),
        P("wide", None),
        P("wide", None),
    )
    return jax.shard_map(
        shards, mesh=mesh, in_specs=placed, out_specs=P(("wide", "narrow"), None), check_vma=False
    )
```

profile of v0, /device:TPU:1, one launch (start us, length us, event | category | flops | bytes accessed | tf_op | source)
XLA Modules:
  0.0 398.9 jit_solution(15326536748898205373)
XLA Ops:
  6.5 0.7 convert_bitcast_fusion
  7.2 0.7 copy.38
  7.9 9.2 %all-to-all-start = ((bf16[16,1,2]{2,1,0:T(2,128)(2,1)}), bf16[16,1,2]{2,1,0:T(2,128)(2,1)S(1)}, u32[]{:S(2)}, u32[]{:S(2)}) async-start(bf16[16,1,2]{2,1,0:T(2,128)(2,1)} %copy.38), calls=%async_computation.1 | async-start | bytes 16384 | tf_op jit(solution)/shard_map/all_to_all | solution.py:75
  17.1 0.7 broadcast_maximum_fusion
  17.8 0.1 copy.40
  17.9 0.1 copy.41
  18.0 0.1 copy.42
  18.1 0.1 reshape.93
  18.2 3.8 gather_fusion
  22.0 6.4 %copy.43 = bf16[32,128,512]{1,2,0:T(8,128)(2,1)} copy(bf16[32,128,512]{2,1,0:T(8,128)(2,1)} %gather_fusion) | data formatting | bytes 8388608 | tf_op jit(solution)/shard_map/jit(_take)/gather | solution.py:69
  28.4 4.7 %select_select_fusion = bf16[16,2,128,512]{2,3,1,0:T(8,128)(2,1)} fusion(bf16[16,2,128,512]{2,3,1,0:T(8,128)(2,1)} %bitcast.57, pred[16,2]{1,0:T(8,128)(4,1)S(1)} %copy.41, pred[16,2]{1,0:T(8,128)(4,1)S(1)} %copy.40), kind=kLoop, calls=%fused_computation.2 | loop fusion | flops 4194304 | bytes 8388672 | tf_op jit(solution)/shard_map/jit(_where)/select_n | solution.py:70
  33.1 0.0 all-to-all-done
  33.1 7.1 %all-to-all-start.1 = ((bf16[16,2,128,512]{2,3,1,0:T(8,128)(2,1)}), bf16[16,2,128,512]{2,3,1,0:T(8,128)(2,1)}, u32[]{:S(2)}, u32[]{:S(2)}) async-start(bf16[16,2,128,512]{2,3,1,0:T(8,128)(2,1)} %select_select_fusion), calls=%async_computation.2 | async-start | bytes 8388608 | tf_op jit(solution)/shard_map/all_to_all | solution.py:74
  40.2 0.0 copy-start.2
  40.3 0.0 reduce-scatter.2.cloned.1.call-start
  40.3 0.2 copy.36
  40.5 0.0 copy-start.4
  40.6 0.1 constant_dynamic-slice_fusion
  40.6 0.7 fusion.20
  42.5 0.2 fusion.9
  42.7 0.0 copy-done.4
  42.7 0.0 copy-start.5
  42.7 0.1 pad_maximum_fusion
  42.8 1.3 copy.37
  44.1 0.0 reduce-scatter.2.cloned.1.call-update
  44.2 0.0 all-gather.4.cloned.1.call-start
  44.2 119.6 %reduce-scatter.2.cloned.1.call-done = bf16[32,512]{1,0:T(8,128)(2,1)} async-done(((bf16[1024,512]{1,0:T(8,128)(2,1)}), bf16[32,512]{1,0:T(8,128)(2,1)}) %reduce-scatter.2.cloned.1.call-update) | async-done | bytes 32784 | tf_op jit(solution)/shard_map/reduce_scatter | solution.py:15
  163.9 0.0 all-gather.4.cloned.1.call-update
  163.9 0.0 all-gather.6.cloned.1.call-start
  163.9 0.7 all-gather.6.cloned.1.call-update
  164.6 0.0 all-gather.8.cloned.1.call-start
  164.7 0.5 all-gather.8.cloned.1.call-update
  165.2 0.3 reduce_sum.29
  165.6 1.8 reduce_sum.27
  167.3 0.1 copy.39
  167.4 0.1 fusion.4
  167.6 0.0 all-to-all-done.1
  167.6 6.7 %convolution_bitcast_fusion = f32[16,2,128,512]{2,3,1,0:T(8,128)} fusion(bf16[16,2,128,512]{2,3,1,0:T(8,128)(2,1)} %all-to-all-done.1, s32[1,16,128,128]{3,2,1,0:T(8,128)S(1)} %copy-done.2), kind=kOutput, calls=%fused_computation.3 | convolution fusion | flops 537133056 | bytes 13631488 | tf_op jit(solution)/shard_map/pij,pcjd->pcid/dot_general | solution.py:22
  174.3 10.4 %copy.44 = f32[16,2,128,512]{3,0,1,2:T(8,128)} copy(f32[16,2,128,512]{2,3,1,0:T(8,128)} %convolution_bitcast_fusion) | data formatting | bytes 16777216 | tf_op jit(solution)/shard_map/pij,pcjd->pcid/transpose | solution.py:22
  184.6 5.6 %convolution_bitcast_fusion.1 = f32[4,128,512]{2,0,1:T(4,128)S(1)} fusion(f32[16,2,128,512]{3,0,1,2:T(8,128)} %copy.44, s32[16,2]{0,1:T(2,128)S(1)} %bitcast.61, pred[16,2]{0,1:T(4,128)(4,1)S(1)} %compare_bitcast_fusion.1), kind=kOutput, calls=%fused_computation.7 | convolution fusion | flops 100663552 | bytes 9437344 | tf_op jit(solution)/shard_map/pcb,pcid->bid/dot_general | solution.py:85
  190.3 0.0 copy-start.3
  190.3 0.3 copy.45
  190.6 1.3 copy.46
  191.9 43.5 %all-gather.4.cloned.1.call-done = bf16[1024,512]{1,0:T(8,128)(2,1)} async-done(((bf16[32,512]{1,0:T(8,128)(2,1)}), bf16[1024,512]{1,0:T(8,128)(2,1)}) %all-gather.4.cloned.1.call-update) | async-done | bytes 1048592 | tf_op jit(solution)/shard_map/all_gather | solution.py:16
  235.4 2.5 fusion.2
  237.9 73.1 %all-gather.6.cloned.1.call-done = bf16[512,2048]{1,0:T(8,128)(2,1)} async-done(((bf16[16,2048]{1,0:T(8,128)(2,1)}), bf16[512,2048]{1,0:T(8,128)(2,1)}) %all-gather.6.cloned.1.call-update) | async-done | bytes 2097168 | tf_op jit(solution)/shard_map/all_gather | solution.py:96
  311.0 76.0 %all-gather.8.cloned.1.call-done = bf16[2048,512]{1,0:T(8,128)(2,1)} async-done(((bf16[64,512]{1,0:T(8,128)(2,1)}), bf16[2048,512]{1,0:T(8,128)(2,1)}) %all-gather.8.cloned.1.call-update) | async-done | bytes 2097168 | tf_op jit(solution)/shard_map/all_gather | solution.py:98
  386.9 5.4 %convolution_convert_fusion = bf16[512,512]{1,0:T(8,128)(2,1)} fusion(bf16[2048,512]{1,0:T(8,128)(2,1)} %all-gather.8.cloned.1.call-done, bf16[512,512]{0,1:T(8,128)(2,1)S(1)} %fusion.2, bf16[512,2048]{1,0:T(8,128)(2,1)} %all-gather.6.cloned.1.call-done), kind=kOutput, calls=%fused_computation.11 | convolution fusion | flops 2149842944 | bytes 5242880 | tf_op jit(solution)/shard_map/dot_general | solution.py:29
  (10 shorter events, 0.0 us)
Async XLA Ops:
  6.5 34.0 %copy-start = (s32[16,2]{0,1:T(2,128)S(1)}, s32[16,2]{0,1:T(2,128)}, u32[]{:S(2)}) copy-start(s32[16,2]{0,1:T(2,128)} %param.9) | copy-start | bytes 388
  7.9 25.2 %all-to-all-start = ((bf16[16,1,2]{2,1,0:T(2,128)(2,1)}), bf16[16,1,2]{2,1,0:T(2,128)(2,1)S(1)}, u32[]{:S(2)}, u32[]{:S(2)}) async-start(bf16[16,1,2]{2,1,0:T(2,128)(2,1)} %copy.38), calls=%async_computation.1 | async-start | bytes 16384 | tf_op jit(solution)/shard_map/all_to_all | solution.py:75
  33.1 7.2 %copy-start.1 = (bf16[512,512]{1,0:T(8,128)(2,1)S(1)}, bf16[512,512]{1,0:T(8,128)(2,1)}, u32[]{:S(2)}) copy-start(bf16[512,512]{1,0:T(8,128)(2,1)} %param.8) | copy-start | bytes 1572868
  33.1 134.5 %all-to-all-start.1 = ((bf16[16,2,128,512]{2,3,1,0:T(8,128)(2,1)}), bf16[16,2,128,512]{2,3,1,0:T(8,128)(2,1)}, u32[]{:S(2)}, u32[]{:S(2)}) async-start(bf16[16,2,128,512]{2,3,1,0:T(8,128)(2,1)} %select_select_fusion), calls=%async_computation.2 | async-start | bytes 8388608 | tf_op jit(solution)/shard_map/all_to_all | solution.py:74
  40.2 125.0 %copy-start.2 = (s32[1,16,128,128]{3,2,1,0:T(8,128)S(1)}, s32[1,16,128,128]{3,2,1,0:T(8,128)}, u32[]{:S(2)}) copy-start(s32[1,16,128,128]{3,2,1,0:T(8,128)} %param.11) | copy-start | bytes 3145732
  40.3 123.6 %reduce-scatter.2.cloned.1.call-start = ((), (), s32[]{:S(2)}) async-start(), calls=%async_computation.3 | async-start | bytes 1081344 | tf_op jit(solution)/shard_map/reduce_scatter | solution.py:15
  40.5 2.2 copy-start.4
  42.7 124.7 %copy-start.5 = (s32[1,16,2]{1,2,0:T(2,128)S(1)}, s32[1,16,2]{1,2,0:T(2,128)}, u32[]{:S(2)}) copy-start(s32[1,16,2]{1,2,0:T(2,128)} %param.13) | copy-start | bytes 388
  44.2 191.2 %all-gather.4.cloned.1.call-start = ((), (), s32[]{:S(2)}) async-start(), calls=%async_computation.4 | async-start | bytes 1081344 | tf_op jit(solution)/shard_map/all_gather | solution.py:16
  163.9 147.1 %all-gather.6.cloned.1.call-start = ((), (), s32[]{:S(2)}) async-start(), calls=%async_computation.5 | async-start | bytes 2162688 | tf_op jit(solution)/shard_map/all_gather | solution.py:96
  164.6 222.3 %all-gather.8.cloned.1.call-start = ((), (), s32[]{:S(2)}) async-start(), calls=%async_computation.6 | async-start | bytes 2162688 | tf_op jit(solution)/shard_map/all_gather | solution.py:98
  190.3 45.1 %copy-start.3 = (s32[512,1024]{1,0:T(8,128)S(1)}, s32[512,1024]{1,0:T(8,128)}, u32[]{:S(2)}) copy-start(s32[512,1024]{1,0:T(8,128)} %param.10) | copy-start | bytes 6291460
Sparse Core Ops, SparseCore 0:
  45.4 118.3 reduce-scatter.1
  167.0 68.3 all-gather.3
  238.5 72.3 all-gather.5
  314.0 72.9 all-gather.7
where the time goes:
time: 400 us; the launch traced here: 399 us
  waiting for transfers between devices  313 us (78%)
  local copies, waits for them, and re-layouts  25.7 us (6%)
  matrix products  20.3 us (5%)
  starting transfers between devices  16.5 us (4%)
  between operations  14.5 us (4%)
  other arithmetic  8.46 us (2%)
    reduce_scatter x1, waiting for transfers between devices, total_of(): own = lax.psum_scatter(padded, axis, scatter_dimension=0, tiled=True)  120 us
    all_gather x1, waiting for transfers between devices, shards(): lax.all_gather(second_weight, 'wide', axis=0, tiled=True)  76 us
    all_gather x1, waiting for transfers between devices, shards(): lax.all_gather(first_weight, 'wide', axis=0, tiled=True)  73.1 us
    all_gather x1, waiting for transfers between devices, total_of(): whole = lax.all_gather(own, axis, axis=0, tiled=True)  43.5 us
    transpose x1, local copies, waits for them, and re-layouts, tile_products(): jnp.einsum('pij,pcjd->pcid', tile_weights, carried, preferred_element_typ...  10.4 us
    gather x2, local copies, waits for them, and re-layouts, shards(): chosen = jnp.take(block_grid, jnp.maximum(listed, 0), axis=0)  10.2 us
    all_to_all x1, starting transfers between devices, shards(): lax.all_to_all(present.astype(jnp.bfloat16), 'narrow', split_axis=0, conc...  9.17 us
  transfers between devices with their start and end apart: 6, of which 4 were waited for; matrix products, arithmetic and copies ran while one was open for 12% of the time, Pallas kernels for 0%

commit v1 on v0

--- a/solution.py
+++ b/solution.py
@@ -95,7 +95,12 @@
     ).astype(jnp.bfloat16)
     gated = add_rows(combined, lax.all_gather(first_weight, "wide", axis=0, tiled=True))
     hidden = jax.nn.relu(gated).astype(jnp.bfloat16)
-    updated = add_rows(hidden, lax.all_gather(second_weight, "wide", axis=0, tiled=True))
+    updated = add_rows(
+        hidden,
+        jnp.concatenate(
+            lax.all_to_all(jnp.stack([second_weight] * lax.axis_size("wide")), "wide", 0, 0), axis=0
+        ),
+    )
     return updated.astype(jnp.bfloat16)
 
 

time: 400 us -> 454 us (1.14)
  waiting for transfers between devices: 313 us -> 349 us
  starting transfers between devices: 16.5 us -> 33.6 us
    all_to_all x1, waiting for transfers between devices: 0.01 us -> 96 us  [shards(): lax.all_to_all(chosen, 'narrow', split_axis=0, concat_axis=0, tiled=True)]
    all_gather x1 -> x0, waiting for transfers between devices: 76 us -> none  [shards(): lax.all_gather(second_weight, 'wide', axis=0, tiled=True)]
    all_to_all x0 -> x1, starting transfers between devices: none -> 17.1 us  [shards(): lax.all_to_all(jnp.stack([second_weight] * lax.axis_size('wide')), 'wide'...]
    reduce_scatter x1, waiting for transfers between devices: 120 us -> 135 us  [total_of(): own = lax.psum_scatter(padded, axis, scatter_dimension=0, tiled=True)]
  transfers between devices with their start and end apart: 6 -> 6, of which waited for: 4 -> 4; matrix products, arithmetic and copies ran while one was open for 12% -> 11% of each run, Pallas kernels for 0% -> 0%
where the time goes in v1:
time: 454 us; the launch traced here: 453 us
  waiting for transfers between devices  349 us (77%)
  starting transfers between devices  33.6 us (7%)
  local copies, waits for them, and re-layouts  27.2 us (6%)
  matrix products  20.3 us (4%)
  between operations  14.5 us (3%)
  other arithmetic  8.48 us (2%)
    reduce_scatter x1, waiting for transfers between devices, total_of(): own = lax.psum_scatter(padded, axis, scatter_dimension=0, tiled=True)  135 us
    all_to_all x1, waiting for transfers between devices, shards(): lax.all_to_all(chosen, 'narrow', split_axis=0, concat_axis=0, tiled=True)  96 us
    all_gather x1, waiting for transfers between devices, shards(): lax.all_gather(first_weight, 'wide', axis=0, tiled=True)  73.1 us
    all_gather x1, waiting for transfers between devices, total_of(): whole = lax.all_gather(own, axis, axis=0, tiled=True)  44.1 us
    all_to_all x1, starting transfers between devices, shards(): lax.all_to_all(jnp.stack([second_weight] * lax.axis_size('wide')), 'wide'...  17.1 us
    transpose x1, local copies, waits for them, and re-layouts, tile_products(): jnp.einsum('pij,pcjd->pcid', tile_weights, carried, preferred_element_typ...  10.4 us
    gather x2, local copies, waits for them, and re-layouts, shards(): chosen = jnp.take(block_grid, jnp.maximum(listed, 0), axis=0)  10.3 us
    all_to_all x1, starting transfers between devices, shards(): lax.all_to_all(present.astype(jnp.bfloat16), 'narrow', split_axis=0, conc...  9.17 us
  transfers between devices with their start and end apart: 6, of which 4 were waited for; matrix products, arithmetic and copies ran while one was open for 11% of the time, Pallas kernels for 0%

profile of v1, /device:TPU:1, one launch (start us, length us, event | category | flops | bytes accessed | tf_op | source)
XLA Modules:
  0.0 453.4 jit_solution(16186135347328983726)
XLA Ops:
  6.5 0.7 convert_bitcast_fusion
  7.2 0.7 copy.38
  7.9 9.2 %all-to-all-start = ((bf16[16,1,2]{2,1,0:T(2,128)(2,1)}), bf16[16,1,2]{2,1,0:T(2,128)(2,1)S(1)}, u32[]{:S(2)}, u32[]{:S(2)}) async-start(bf16[16,1,2]{2,1,0:T(2,128)(2,1)} %copy.38), calls=%async_computation.1 | async-start | bytes 16384 | tf_op jit(solution)/shard_map/all_to_all | solution.py:75
  17.1 0.7 broadcast_maximum_fusion
  17.8 0.1 copy.40
  17.9 0.1 copy.41
  18.0 0.1 copy.42
  18.1 0.1 reshape.99
  18.2 3.8 gather_fusion
  22.0 6.4 %copy.43 = bf16[32,128,512]{1,2,0:T(8,128)(2,1)} copy(bf16[32,128,512]{2,1,0:T(8,128)(2,1)} %gather_fusion) | data formatting | bytes 8388608 | tf_op jit(solution)/shard_map/jit(_take)/gather | solution.py:69
  28.4 4.7 %select_select_fusion = bf16[16,2,128,512]{2,3,1,0:T(8,128)(2,1)} fusion(bf16[16,2,128,512]{2,3,1,0:T(8,128)(2,1)} %bitcast.58, pred[16,2]{1,0:T(8,128)(4,1)S(1)} %copy.41, pred[16,2]{1,0:T(8,128)(4,1)S(1)} %copy.40), kind=kLoop, calls=%fused_computation.2 | loop fusion | flops 4194304 | bytes 8388672 | tf_op jit(solution)/shard_map/jit(_where)/select_n | solution.py:70
  33.1 0.0 all-to-all-done
  33.1 7.1 %all-to-all-start.1 = ((bf16[16,2,128,512]{2,3,1,0:T(8,128)(2,1)}), bf16[16,2,128,512]{2,3,1,0:T(8,128)(2,1)}, u32[]{:S(2)}, u32[]{:S(2)}) async-start(bf16[16,2,128,512]{2,3,1,0:T(8,128)(2,1)} %select_select_fusion), calls=%async_computation.2 | async-start | bytes 8388608 | tf_op jit(solution)/shard_map/all_to_all | solution.py:74
  40.3 0.0 copy-start.1
  40.3 0.1 constant_dynamic-slice_fusion
  40.4 96.0 %all-to-all-done.1 = bf16[16,2,128,512]{2,3,1,0:T(8,128)(2,1)} async-done(((bf16[16,2,128,512]{2,3,1,0:T(8,128)(2,1)}), bf16[16,2,128,512]{2,3,1,0:T(8,128)(2,1)}, u32[]{:S(2)}, u32[]{:S(2)}) %all-to-all-start.1) | async-done | bytes 4194336 | tf_op jit(solution)/shard_map/all_to_all | solution.py:74
  136.4 1.5 stack.14
  137.9 17.1 %all-to-all-start.2 = ((bf16[32,64,512]{2,1,0:T(8,128)(2,1)}), bf16[32,64,512]{2,1,0:T(8,128)(2,1)}, u32[]{:S(2)}, u32[]{:S(2)}) async-start(bf16[32,64,512]{2,1,0:T(8,128)(2,1)} %stack.14), calls=%async_computation.3 | async-start | bytes 4194304 | tf_op jit(solution)/shard_map/all_to_all | solution.py:101
  155.1 0.0 copy-start.2
  155.1 0.0 reduce-scatter.2.cloned.1.call-start
  155.2 0.5 fusion.20
  155.7 0.2 copy.36
  155.9 0.0 copy-start.4
  157.2 0.2 fusion.9
  157.4 0.0 copy-start.6
  157.4 0.1 pad_maximum_fusion
  157.5 1.4 copy.37
  158.8 0.0 reduce-scatter.2.cloned.1.call-update
  158.9 0.0 all-gather.3.cloned.1.call-start
  158.9 135.5 %reduce-scatter.2.cloned.1.call-done = bf16[32,512]{1,0:T(8,128)(2,1)} async-done(((bf16[1024,512]{1,0:T(8,128)(2,1)}), bf16[32,512]{1,0:T(8,128)(2,1)}) %reduce-scatter.2.cloned.1.call-update) | async-done | bytes 32784 | tf_op jit(solution)/shard_map/reduce_scatter | solution.py:15
  294.4 0.0 all-gather.3.cloned.1.call-update
  294.4 0.0 all-gather.5.cloned.1.call-start
  294.4 0.7 all-gather.5.cloned.1.call-update
  295.1 0.3 reduce_sum.29
  295.5 1.8 reduce_sum.27
  297.3 0.1 copy.39
  297.4 0.1 fusion.4
  297.5 6.7 %convolution_bitcast_fusion = f32[16,2,128,512]{2,3,1,0:T(8,128)} fusion(bf16[16,2,128,512]{2,3,1,0:T(8,128)(2,1)} %all-to-all-done.1, s32[1,16,128,128]{3,2,1,0:T(8,128)S(1)} %copy-done.2), kind=kOutput, calls=%fused_computation.3 | convolution fusion | flops 537133056 | bytes 13631488 | tf_op jit(solution)/shard_map/pij,pcjd->pcid/dot_general | solution.py:22
  304.2 10.4 %copy.44 = f32[16,2,128,512]{3,0,1,2:T(8,128)} copy(f32[16,2,128,512]{2,3,1,0:T(8,128)} %convolution_bitcast_fusion) | data formatting | bytes 16777216 | tf_op jit(solution)/shard_map/pij,pcjd->pcid/transpose | solution.py:22
  314.6 5.6 %convolution_bitcast_fusion.1 = f32[4,128,512]{2,0,1:T(4,128)S(1)} fusion(f32[16,2,128,512]{3,0,1,2:T(8,128)} %copy.44, s32[16,2]{0,1:T(2,128)S(1)} %bitcast.62, pred[16,2]{0,1:T(4,128)(4,1)S(1)} %compare_bitcast_fusion.1), kind=kOutput, calls=%fused_computation.7 | convolution fusion | flops 100663552 | bytes 9437344 | tf_op jit(solution)/shard_map/pcb,pcid->bid/dot_general | solution.py:85
  320.2 0.0 copy-start.3
  320.2 0.3 copy.45
  320.5 1.3 copy.46
  321.9 44.1 %all-gather.3.cloned.1.call-done = bf16[1024,512]{1,0:T(8,128)(2,1)} async-done(((bf16[32,512]{1,0:T(8,128)(2,1)}), bf16[1024,512]{1,0:T(8,128)(2,1)}) %all-gather.3.cloned.1.call-update) | async-done | bytes 1048592 | tf_op jit(solution)/shard_map/all_gather | solution.py:16
  365.9 2.5 fusion.2
  368.4 73.1 %all-gather.5.cloned.1.call-done = bf16[512,2048]{1,0:T(8,128)(2,1)} async-done(((bf16[16,2048]{1,0:T(8,128)(2,1)}), bf16[512,2048]{1,0:T(8,128)(2,1)}) %all-gather.5.cloned.1.call-update) | async-done | bytes 2097168 | tf_op jit(solution)/shard_map/all_gather | solution.py:96
  441.5 0.0 all-to-all-done.2
  441.5 5.4 %convolution_convert_fusion = bf16[512,512]{1,0:T(8,128)(2,1)} fusion(bf16[2048,512]{1,0:T(8,128)(2,1)} %bitcast.22, bf16[512,512]{0,1:T(8,128)(2,1)S(1)} %fusion.2, bf16[512,2048]{1,0:T(8,128)(2,1)} %all-gather.5.cloned.1.call-done), kind=kOutput, calls=%fused_computation.11 | convolution fusion | flops 2149842944 | bytes 5242880 | tf_op jit(solution)/shard_map/dot_general | solution.py:29
  (12 shorter events, 0.0 us)
Async XLA Ops:
  6.5 33.8 %copy-start = (s32[16,2]{0,1:T(2,128)S(1)}, s32[16,2]{0,1:T(2,128)}, u32[]{:S(2)}) copy-start(s32[16,2]{0,1:T(2,128)} %param.9) | copy-start | bytes 388
  7.9 25.2 %all-to-all-start = ((bf16[16,1,2]{2,1,0:T(2,128)(2,1)}), bf16[16,1,2]{2,1,0:T(2,128)(2,1)S(1)}, u32[]{:S(2)}, u32[]{:S(2)}) async-start(bf16[16,1,2]{2,1,0:T(2,128)(2,1)} %copy.38), calls=%async_computation.1 | async-start | bytes 16384 | tf_op jit(solution)/shard_map/all_to_all | solution.py:75
  33.1 103.3 %copy-start.5 = (bf16[64,512]{1,0:T(8,128)(2,1)S(1)}, bf16[64,512]{1,0:T(8,128)(2,1)}, u32[]{:S(2)}) copy-start(bf16[64,512]{1,0:T(8,128)(2,1)} %param.15) | copy-start | bytes 196612
  33.1 103.3 %all-to-all-start.1 = ((bf16[16,2,128,512]{2,3,1,0:T(8,128)(2,1)}), bf16[16,2,128,512]{2,3,1,0:T(8,128)(2,1)}, u32[]{:S(2)}, u32[]{:S(2)}) async-start(bf16[16,2,128,512]{2,3,1,0:T(8,128)(2,1)} %select_select_fusion), calls=%async_computation.2 | async-start | bytes 8388608 | tf_op jit(solution)/shard_map/all_to_all | solution.py:74
  40.3 115.4 %copy-start.1 = (bf16[512,512]{1,0:T(8,128)(2,1)S(1)}, bf16[512,512]{1,0:T(8,128)(2,1)}, u32[]{:S(2)}) copy-start(bf16[512,512]{1,0:T(8,128)(2,1)} %param.8) | copy-start | bytes 1572868
  137.9 303.6 %all-to-all-start.2 = ((bf16[32,64,512]{2,1,0:T(8,128)(2,1)}), bf16[32,64,512]{2,1,0:T(8,128)(2,1)}, u32[]{:S(2)}, u32[]{:S(2)}) async-start(bf16[32,64,512]{2,1,0:T(8,128)(2,1)} %stack.14), calls=%async_computation.3 | async-start | bytes 4194304 | tf_op jit(solution)/shard_map/all_to_all | solution.py:101
  155.1 140.0 %copy-start.2 = (s32[1,16,128,128]{3,2,1,0:T(8,128)S(1)}, s32[1,16,128,128]{3,2,1,0:T(8,128)}, u32[]{:S(2)}) copy-start(s32[1,16,128,128]{3,2,1,0:T(8,128)} %param.11) | copy-start | bytes 3145732
  155.1 139.3 %reduce-scatter.2.cloned.1.call-start = ((), (), s32[]{:S(2)}) async-start(), calls=%async_computation.4 | async-start | bytes 1081344 | tf_op jit(solution)/shard_map/reduce_scatter | solution.py:15
  155.9 1.4 copy-start.4
  157.4 140.0 %copy-start.6 = (s32[1,16,2]{1,2,0:T(2,128)S(1)}, s32[1,16,2]{1,2,0:T(2,128)}, u32[]{:S(2)}) copy-start(s32[1,16,2]{1,2,0:T(2,128)} %param.13) | copy-start | bytes 388
  158.9 207.1 %all-gather.3.cloned.1.call-start = ((), (), s32[]{:S(2)}) async-start(), calls=%async_computation.5 | async-start | bytes 1081344 | tf_op jit(solution)/shard_map/all_gather | solution.py:16
  294.4 147.1 %all-gather.5.cloned.1.call-start = ((), (), s32[]{:S(2)}) async-start(), calls=%async_computation.6 | async-start | bytes 2162688 | tf_op jit(solution)/shard_map/all_gather | solution.py:96
  320.2 45.7 %copy-start.3 = (s32[512,1024]{1,0:T(8,128)S(1)}, s32[512,1024]{1,0:T(8,128)}, u32[]{:S(2)}) copy-start(s32[512,1024]{1,0:T(8,128)} %param.10) | copy-start | bytes 6291460
Sparse Core Ops, SparseCore 0:
  160.3 134.0 reduce-scatter.1
  297.5 68.3 all-gather.2
  369.1 72.3 all-gather.4
